TPU v7x, 256 devices: a whole 4x4x8 slice. The times are simulated.
256 devices in a mesh: pipe: 8 (over x, core), dp: 32 (over z, y).
Axes of the slice: x: 4, y: 4, z: 8, core: 2. Of those that a mesh axis runs over, the one named last changes fastest.
Arguments:
- x_ckpt: bfloat16 [8, 2, 32, 512, 512], P('pipe', None, 'dp'), may hold values from -6 to 6
- top_cot: bfloat16 [2, 32, 512, 512], P(None, 'dp'), may hold values from -6 to 6
- skip_cot: bfloat16 [2, 32, 512, 512], P(None, 'dp'), may hold values from -6 to 6
- w_conv: bfloat16 [8, 512, 3, 1024], P('pipe', 'dp'), may hold values from -0.15625 to 0.15625
- w_mix: bfloat16 [8, 512, 1024], P('pipe', 'dp'), may hold values from -0.25 to 0.25
Outputs:
- cot_inputs: bfloat16 [8, 2, 32, 512, 512], P('pipe', None, 'dp')
- grad_conv: float32 [8, 512, 3, 1024], P('pipe', 'dp')
- grad_mix: float32 [8, 512, 1024], P('pipe', 'dp')
All inputs are finite; a program needn't handle non-finite values.
Results may differ from a plain program's by a relative error of at most 0.014.
Values may be sent and summed in bfloat16 or wider, within the bound.
A program may use at most 128 MiB of HBM per device.

v0:
```python
import jax
import jax.numpy as jnp
from jax import lax
from jax.sharding import PartitionSpec as P


def passed_along(value, axis, steps):
    count = lax.axis_size(axis)
    leading, last = (max(0, -steps), min(count, count - steps))
    return lax.ppermute(value, axis, [(source, source + steps) for source in range(leading, last)])


def delay_seq(signal, shift_by):
    samples = signal.shape[1]
    rolled = jnp.roll(signal, shift_by, axis=1)
    positions = lax.broadcasted_iota(jnp.int32, (1, samples, 1), 1)
    return jnp.where(positions >= shift_by, rolled, jnp.zeros_like(rolled))


def advance_seq(signal, shift_by):
    samples = signal.shape[1]
    rolled = jnp.roll(signal, -shift_by, axis=1)
    positions = lax.broadcasted_iota(jnp.int32, (1, samples, 1), 1)
    return jnp.where(positions < samples - shift_by, rolled, jnp.zeros_like(rolled))


def tap_stack(signal, dilation):
    return jnp.stack([delay_seq(signal, offset * dilation) for offset in range(3)], axis=2)


def layer_back(x_rows, grad_next, skip_grad, conv_w, mix_w, dilation):
    channels = x_rows.shape[2]
    tapped_x = tap_stack(x_rows, dilation)
    pre_act = jnp.einsum("slkc,ckn->sln", tapped_x, conv_w, preferred_element_type=jnp.float32)
    filter_act = jnp.tanh(pre_act[..., :channels])
    gate_act = jax.nn.sigmoid(pre_act[..., channels:])
    hidden = (filter_act * gate_act).astype(jnp.bfloat16)
    cot_pair = jnp.concatenate([grad_next, skip_grad], axis=2)
    hid_grad = jnp.einsum("sln,cn->slc", cot_pair, mix_w, preferred_element_type=jnp.float32)
    pre_grad = jnp.concatenate(
        [
            hid_grad * gate_act * (1.0 - filter_act * filter_act),
            hid_grad * filter_act * gate_act * (1.0 - gate_act),
        ],
        axis=2,
    ).astype(jnp.bfloat16)
    back_taps = jnp.einsum("sln,ckn->slkc", pre_grad, conv_w, preferred_element_type=jnp.float32)
    input_grad = grad_next.astype(jnp.float32)
    for offset in range(3):
        input_grad = input_grad + advance_seq(back_taps[:, :, offset], offset * dilation)
    return (input_grad.astype(jnp.bfloat16), tapped_x, hidden, pre_grad, cot_pair)


def weight_terms(tapped_x, hidden, pre_grad, cot_pair):
    conv_term = jnp.einsum("slkc,sln->ckn", tapped_x, pre_grad, preferred_element_type=jnp.float32)
    mix_term = jnp.einsum("slc,sln->cn", hidden, cot_pair, preferred_element_type=jnp.float32)
    return jnp.concatenate([conv_term.reshape(conv_term.shape[0], -1), mix_term], axis=1)


def local(x_ckpt, top_cot, skip_cot, w_conv, w_mix):
    sec_count = lax.axis_size("pipe")
    sec_index = lax.axis_index("pipe")
    dilation = jnp.left_shift(jnp.int32(1), sec_index)
    conv_full, mix_full = (
        lax.all_gather(w_conv, "dp", axis=1, tiled=True),
        lax.all_gather(w_mix, "dp", axis=1, tiled=True),
    )
    conv_w = conv_full[0]
    mix_w = mix_full[0]
    micro_count, seq_count, samples, channels = x_ckpt.shape[1:]
    all_rows = micro_count * seq_count
    x_rows = x_ckpt[0].reshape(all_rows, samples, channels)
    top_rows = top_cot.reshape(all_rows, samples, channels)
    skip_rows = skip_cot.reshape(all_rows, samples, channels)
    is_last = sec_index == sec_count - 1
    blk_count = all_rows // seq_count
    step_count = sec_count + blk_count - 1
    act_shape = (seq_count, samples, channels)
    pair_shape = (seq_count, samples, 2 * channels)
    grad_init = jnp.zeros((channels, 8 * channels), jnp.float32)
    hid_init = jnp.zeros((1,), jnp.bfloat16)
    pre_init = jnp.zeros((1,), jnp.bfloat16)
    pair_init = jnp.zeros((1,), jnp.bfloat16)

    def step_fn(step_no, state_tuple):
        received, cot_store, grad_acc, hid_store, pre_store, pair_store = state_tuple
        blk_index = step_no - (sec_count - 1 - sec_index)
        is_active = (blk_index >= 0) & (blk_index < blk_count)
        row_start = jnp.clip(blk_index, 0, blk_count - 1) * seq_count
        x_blk = lax.dynamic_slice_in_dim(x_rows, row_start, seq_count, 0)
        top_blk = lax.dynamic_slice_in_dim(top_rows, row_start, seq_count, 0)
        skip_blk = lax.dynamic_slice_in_dim(skip_rows, row_start, seq_count, 0)
        grad_next = jnp.where(is_last, top_blk, received)

        def do_work(unused):
            input_grad, tapped_x, hidden, pre_grad, cot_pair = layer_back(
                x_blk, grad_next, skip_blk, conv_w, mix_w, dilation
            )
            grad_term = weight_terms(tapped_x, hidden, pre_grad, cot_pair)
            return (input_grad, hidden, pre_grad, cot_pair, grad_term)

        def no_work(unused):
            return (
                jnp.zeros(act_shape, jnp.bfloat16),
                jnp.zeros(act_shape, jnp.bfloat16),
                jnp.zeros(pair_shape, jnp.bfloat16),
                jnp.zeros(pair_shape, jnp.bfloat16),
                jnp.zeros_like(grad_acc),
            )

        input_grad, hidden, pre_grad, cot_pair, grad_term = lax.cond(is_active, do_work, no_work, 0)
        grad_acc = grad_acc + grad_term
        cot_store = jnp.where(
            is_active,
            lax.dynamic_update_slice_in_dim(cot_store, input_grad, row_start, 0),
            cot_store,
        )
        received = passed_along(input_grad, "pipe", -1)
        return (received, cot_store, grad_acc, hid_store, pre_store, pair_store)

    initial = (
        jnp.zeros(act_shape, jnp.bfloat16),
        jnp.zeros((all_rows, samples, channels), jnp.bfloat16),
        grad_init,
        hid_init,
        pre_init,
        pair_init,
    )
    final_state = lax.fori_loop(0, step_count, step_fn, initial)
    cot_store, grad_acc, hid_store, pre_store, pair_store = final_state[1:]
    shard_rows = channels // lax.axis_size("dp")
    shares = lax.psum_scatter(grad_acc, "dp", scatter_dimension=0, tiled=True)
    conv_share = shares[:, : 6 * channels].reshape(shard_rows, 3, 2 * channels)
    mix_share = shares[:, 6 * channels :]
    return (
        cot_store.reshape(1, micro_count, seq_count, samples, channels),
        conv_share[None],
        mix_share[None],
    )


def solution(mesh):
    placed = (
        P("pipe", None, "dp", None, None),
        P(None, "dp", None, None),
        P(None, "dp", None, None),
        P("pipe", "dp", None, None),
        P("pipe", "dp", None),
    )
    return jax.shard_map(
        local,
        mesh=mesh,
        in_specs=placed,
        out_specs=(
            P("pipe", None, "dp", None, None),
            P("pipe", "dp", None, None),
            P("pipe", "dp", None),
        ),
        check_vma=False,
    )
```

profile of v0, /device:TPU:2, one launch (start us, length us, event | category | flops | bytes accessed | tf_op | source)
XLA Modules:
  0.0 634.7 jit_solution(10756008087756776390)
XLA Ops:
  8.7 81.3 %all-gather.3.cloned.1.call-done = bf16[1,512,1024]{2,1,0:T(8,128)(2,1)} async-done(((bf16[1,16,1024]{2,1,0:T(8,128)(2,1)}), bf16[1,512,1024]{2,1,0:T(8,128)(2,1)}) %all-gather.3.cloned.1.call-update) | async-done | bytes 1048592 | tf_op jit(solution)/shard_map/all_gather | solution.py:66
  90.0 79.5 %all-gather.5.cloned.1.call-done = bf16[1,512,3,1024]{3,1,2,0:T(8,128)(2,1)} async-done(((bf16[1,16,3,1024]{3,1,2,0:T(8,128)(2,1)}), bf16[1,512,3,1024]{3,1,2,0:T(8,128)(2,1)}) %all-gather.5.cloned.1.call-update) | async-done | bytes 3145744 | tf_op jit(solution)/shard_map/all_gather | solution.py:65
  170.6 218.1 %while.20 = (s32[]{:T(128)}, bf16[1,512,512]{2,1,0:T(8,128)(2,1)S(1)}, bf16[2,512,512]{2,1,0:T(8,128)(2,1)}, f32[512,4096]{0,1:T(8,128)}, s32[]{:T(128)}, /*inde...) while((s32[]{:T(128)}, ...), condition=%wide.region_3.8_spmd.clone, body=%wide.region_0.7_spmd.clone.sunk | while | flops 5937039872 | bytes 117971056 | solution.py:129
  170.6 4.3 conditional.3
  176.8 8.8 %select_add_fusion.2 = f32[512,4096]{0,1:T(8,128)} fusion(f32[512,4096]{0,1:T(8,128)} %get-tuple-element.522, f32[512,4096]{0,1:T(8,128)} %get-tuple-element.545, pred[]{:T(512)S(6)} %compare.5), kind=kLoop, calls=%fused_computation.59.clone.1 | loop fusion | flops 4194304 | bytes 25165824 | tf_op jit(solution)/shard_map/while/body/eval_jaxpr/add | solution.py:112
  186.8 4.3 conditional.3
  193.7 11.2 %select_add_fusion.2 = f32[512,4096]{0,1:T(8,128)} fusion(f32[512,4096]{0,1:T(8,128)} %get-tuple-element.522, f32[512,4096]{0,1:T(8,128)} %get-tuple-element.545, pred[]{:T(512)S(6)} %compare.5), kind=kLoop, calls=%fused_computation.59.clone.1 | loop fusion | flops 4194304 | bytes 25165824 | tf_op jit(solution)/shard_map/while/body/eval_jaxpr/add | solution.py:112
  206.1 4.3 conditional.3
  212.4 11.2 %select_add_fusion.2 = f32[512,4096]{0,1:T(8,128)} fusion(f32[512,4096]{0,1:T(8,128)} %get-tuple-element.522, f32[512,4096]{0,1:T(8,128)} %get-tuple-element.545, pred[]{:T(512)S(6)} %compare.5), kind=kLoop, calls=%fused_computation.59.clone.1 | loop fusion | flops 4194304 | bytes 25165824 | tf_op jit(solution)/shard_map/while/body/eval_jaxpr/add | solution.py:112
  224.7 4.3 conditional.3
  231.0 11.2 %select_add_fusion.2 = f32[512,4096]{0,1:T(8,128)} fusion(f32[512,4096]{0,1:T(8,128)} %get-tuple-element.522, f32[512,4096]{0,1:T(8,128)} %get-tuple-element.545, pred[]{:T(512)S(6)} %compare.5), kind=kLoop, calls=%fused_computation.59.clone.1 | loop fusion | flops 4194304 | bytes 25165824 | tf_op jit(solution)/shard_map/while/body/eval_jaxpr/add | solution.py:112
  243.4 4.3 conditional.3
  249.7 11.2 %select_add_fusion.2 = f32[512,4096]{0,1:T(8,128)} fusion(f32[512,4096]{0,1:T(8,128)} %get-tuple-element.522, f32[512,4096]{0,1:T(8,128)} %get-tuple-element.545, pred[]{:T(512)S(6)} %compare.5), kind=kLoop, calls=%fused_computation.59.clone.1 | loop fusion | flops 4194304 | bytes 25165824 | tf_op jit(solution)/shard_map/while/body/eval_jaxpr/add | solution.py:112
  261.0 19.7 %collective-permute-done = bf16[1,512,512]{2,1,0:T(8,128)(2,1)S(1)} collective-permute-done((bf16[1,512,512]{2,1,0:T(8,128)(2,1)S(1)}, bf16[1,512,512]{2,1,0:T(8,128)(2,1)S(1)}, u32[]{:S(2)}, u32[]{:S(2)}) %collective-permute-start) | collective-permute-done | bytes 524320 | tf_op jit(solution)/shard_map/while/body/eval_jaxpr/ppermute | solution.py:10
  280.8 16.7 %conditional.3 = (bf16[1,512,512]{2,1,0:T(8,128)(2,1)S(1)}, f32[512,4096]{0,1:T(8,128)}) conditional(s32[]{:T(128)} %convert_element_type.39, () %tuple.71, (pred[]{:T(512)}, bf16[2,512,512]{2,1,0:T(8,128)(2,1)}, s32[]{:T(128)}, bf16[1,512,512]{2,1,0:T(8,128)(2,1)S(1)}, bf16[2,512,512]{2,1,0:T(8,128)(2,1)}, /*index=5*/bf16[512,1024]{1,0:T(8,128)(2,1)}, ...), branch_computations={%region_1.1_spmd, %region_2.6_spmd} | conditional | flops 5932583424 | bytes 80746224 | solution.py:111
  299.5 11.2 %select_add_fusion.2 = f32[512,4096]{0,1:T(8,128)} fusion(f32[512,4096]{0,1:T(8,128)} %get-tuple-element.522, f32[512,4096]{0,1:T(8,128)} %get-tuple-element.545, pred[]{:T(512)S(6)} %compare.5), kind=kLoop, calls=%fused_computation.59.clone.1 | loop fusion | flops 4194304 | bytes 25165824 | tf_op jit(solution)/shard_map/while/body/eval_jaxpr/add | solution.py:112
  311.8 16.7 %conditional.3 = (bf16[1,512,512]{2,1,0:T(8,128)(2,1)S(1)}, f32[512,4096]{0,1:T(8,128)}) conditional(s32[]{:T(128)} %convert_element_type.39, () %tuple.71, (pred[]{:T(512)}, bf16[2,512,512]{2,1,0:T(8,128)(2,1)}, s32[]{:T(128)}, bf16[1,512,512]{2,1,0:T(8,128)(2,1)S(1)}, bf16[2,512,512]{2,1,0:T(8,128)(2,1)}, /*index=5*/bf16[512,1024]{1,0:T(8,128)(2,1)}, ...), branch_computations={%region_1.1_spmd, %region_2.6_spmd} | conditional | flops 5932583424 | bytes 80746224 | solution.py:111
  330.5 11.2 %select_add_fusion.2 = f32[512,4096]{0,1:T(8,128)} fusion(f32[512,4096]{0,1:T(8,128)} %get-tuple-element.522, f32[512,4096]{0,1:T(8,128)} %get-tuple-element.545, pred[]{:T(512)S(6)} %compare.5), kind=kLoop, calls=%fused_computation.59.clone.1 | loop fusion | flops 4194304 | bytes 25165824 | tf_op jit(solution)/shard_map/while/body/eval_jaxpr/add | solution.py:112
  342.8 4.3 conditional.3
  347.2 10.5 %collective-permute-start = (bf16[1,512,512]{2,1,0:T(8,128)(2,1)S(1)}, bf16[1,512,512]{2,1,0:T(8,128)(2,1)S(1)}, u32[]{:S(2)}, u32[]{:S(2)}) collective-permute-start(bf16[1,512,512]{2,1,0:T(8,128)(2,1)S(1)} %get-tuple-element.521), channel_id=1, source_target_pairs={{32,0},{64,32},{96,64},{128,96},{160,128},{192,160},{224,192},{33,... | collective-permute-start | bytes 1572872 | tf_op jit(solution)/shard_map/while/body/eval_jaxpr/ppermute | solution.py:10
  357.7 11.2 %select_add_fusion.2 = f32[512,4096]{0,1:T(8,128)} fusion(f32[512,4096]{0,1:T(8,128)} %get-tuple-element.522, f32[512,4096]{0,1:T(8,128)} %get-tuple-element.545, pred[]{:T(512)S(6)} %compare.5), kind=kLoop, calls=%fused_computation.59.clone.1 | loop fusion | flops 4194304 | bytes 25165824 | tf_op jit(solution)/shard_map/while/body/eval_jaxpr/add | solution.py:112
  376.3 11.2 %select_add_fusion.2 = f32[512,4096]{0,1:T(8,128)} fusion(f32[512,4096]{0,1:T(8,128)} %get-tuple-element.522, f32[512,4096]{0,1:T(8,128)} %get-tuple-element.545, pred[]{:T(512)S(6)} %compare.5), kind=kLoop, calls=%fused_computation.59.clone.1 | loop fusion | flops 4194304 | bytes 25165824 | tf_op jit(solution)/shard_map/while/body/eval_jaxpr/add | solution.py:112
  388.7 8.9 %copy.15 = f32[512,4096]{1,0:T(8,128)} copy(f32[512,4096]{0,1:T(8,128)} %get-tuple-element.365) | data formatting | bytes 16777216 | tf_op jit(solution)/shard_map/while | solution.py:129
  397.6 227.2 %reduce-scatter.2.cloned.1.call-done = f32[16,4096]{1,0:T(8,128)} async-done(((f32[512,4096]{1,0:T(8,128)}), f32[16,4096]{1,0:T(8,128)}) %reduce-scatter.2.cloned.1.call-update) | async-done | bytes 262160 | tf_op jit(solution)/shard_map/reduce_scatter | solution.py:132
  (125 shorter events, 99.2 us)
Async XLA Ops:
  7.2 82.8 %all-gather.3.cloned.1.call-start = ((), (), s32[]{:S(2)}) async-start(), calls=%async_computation.1 | async-start | bytes 1081344 | tf_op jit(solution)/shard_map/all_gather | solution.py:66
  7.9 161.6 %all-gather.5.cloned.1.call-start = ((), (), s32[]{:S(2)}) async-start(), calls=%async_computation.2 | async-start | bytes 3244032 | tf_op jit(solution)/shard_map/all_gather | solution.py:65
  8.6 616.2 %reduce-scatter.2.cloned.1.call-start = ((), (), s32[]{:S(2)}) async-start(), calls=%async_computation.3 | async-start | bytes 8650752 | tf_op jit(solution)/shard_map/reduce_scatter | solution.py:132
  174.9 11.0 %collective-permute-start = (bf16[1,512,512]{2,1,0:T(8,128)(2,1)S(1)}, bf16[1,512,512]{2,1,0:T(8,128)(2,1)S(1)}, u32[]{:S(2)}, u32[]{:S(2)}) collective-permute-start(bf16[1,512,512]{2,1,0:T(8,128)(2,1)S(1)} %get-tuple-element.521), channel_id=1, source_target_pairs={{32,0},{64,32},{96,64},{128,96},{160,128},{192,160},{224,192},{33,... | collective-permute-start | bytes 1572872 | tf_op jit(solution)/shard_map/while/body/eval_jaxpr/ppermute | solution.py:10
  176.8 8.8 %copy-start = (bf16[2,512,512]{2,1,0:T(8,128)(2,1)S(1)}, bf16[2,512,512]{2,1,0:T(8,128)(2,1)}, u32[]{:S(2)}) copy-start(bf16[2,512,512]{2,1,0:T(8,128)(2,1)} %get-tuple-element.544) | copy-start | bytes 3145732 | tf_op jit(solution)/shard_map/while
  191.2 14.0 %collective-permute-start = (bf16[1,512,512]{2,1,0:T(8,128)(2,1)S(1)}, bf16[1,512,512]{2,1,0:T(8,128)(2,1)S(1)}, u32[]{:S(2)}, u32[]{:S(2)}) collective-permute-start(bf16[1,512,512]{2,1,0:T(8,128)(2,1)S(1)} %get-tuple-element.521), channel_id=1, source_target_pairs={{32,0},{64,32},{96,64},{128,96},{160,128},{192,160},{224,192},{33,... | collective-permute-start | bytes 1572872 | tf_op jit(solution)/shard_map/while/body/eval_jaxpr/ppermute | solution.py:10
  193.7 11.2 %copy-start = (bf16[2,512,512]{2,1,0:T(8,128)(2,1)S(1)}, bf16[2,512,512]{2,1,0:T(8,128)(2,1)}, u32[]{:S(2)}) copy-start(bf16[2,512,512]{2,1,0:T(8,128)(2,1)} %get-tuple-element.544) | copy-start | bytes 3145732 | tf_op jit(solution)/shard_map/while
  210.4 13.3 %collective-permute-start = (bf16[1,512,512]{2,1,0:T(8,128)(2,1)S(1)}, bf16[1,512,512]{2,1,0:T(8,128)(2,1)S(1)}, u32[]{:S(2)}, u32[]{:S(2)}) collective-permute-start(bf16[1,512,512]{2,1,0:T(8,128)(2,1)S(1)} %get-tuple-element.521), channel_id=1, source_target_pairs={{32,0},{64,32},{96,64},{128,96},{160,128},{192,160},{224,192},{33,... | collective-permute-start | bytes 1572872 | tf_op jit(solution)/shard_map/while/body/eval_jaxpr/ppermute | solution.py:10
  212.4 11.2 %copy-start = (bf16[2,512,512]{2,1,0:T(8,128)(2,1)S(1)}, bf16[2,512,512]{2,1,0:T(8,128)(2,1)}, u32[]{:S(2)}) copy-start(bf16[2,512,512]{2,1,0:T(8,128)(2,1)} %get-tuple-element.544) | copy-start | bytes 3145732 | tf_op jit(solution)/shard_map/while
  229.1 13.3 %collective-permute-start = (bf16[1,512,512]{2,1,0:T(8,128)(2,1)S(1)}, bf16[1,512,512]{2,1,0:T(8,128)(2,1)S(1)}, u32[]{:S(2)}, u32[]{:S(2)}) collective-permute-start(bf16[1,512,512]{2,1,0:T(8,128)(2,1)S(1)} %get-tuple-element.521), channel_id=1, source_target_pairs={{32,0},{64,32},{96,64},{128,96},{160,128},{192,160},{224,192},{33,... | collective-permute-start | bytes 1572872 | tf_op jit(solution)/shard_map/while/body/eval_jaxpr/ppermute | solution.py:10
  231.0 11.2 %copy-start = (bf16[2,512,512]{2,1,0:T(8,128)(2,1)S(1)}, bf16[2,512,512]{2,1,0:T(8,128)(2,1)}, u32[]{:S(2)}) copy-start(bf16[2,512,512]{2,1,0:T(8,128)(2,1)} %get-tuple-element.544) | copy-start | bytes 3145732 | tf_op jit(solution)/shard_map/while
  247.7 33.1 %collective-permute-start = (bf16[1,512,512]{2,1,0:T(8,128)(2,1)S(1)}, bf16[1,512,512]{2,1,0:T(8,128)(2,1)S(1)}, u32[]{:S(2)}, u32[]{:S(2)}) collective-permute-start(bf16[1,512,512]{2,1,0:T(8,128)(2,1)S(1)} %get-tuple-element.521), channel_id=1, source_target_pairs={{32,0},{64,32},{96,64},{128,96},{160,128},{192,160},{224,192},{33,... | collective-permute-start | bytes 1572872 | tf_op jit(solution)/shard_map/while/body/eval_jaxpr/ppermute | solution.py:10
  249.6 11.2 %copy-start = (bf16[2,512,512]{2,1,0:T(8,128)(2,1)S(1)}, bf16[2,512,512]{2,1,0:T(8,128)(2,1)}, u32[]{:S(2)}) copy-start(bf16[2,512,512]{2,1,0:T(8,128)(2,1)} %get-tuple-element.544) | copy-start | bytes 3145732 | tf_op jit(solution)/shard_map/while
  261.0 19.7 %copy-start.1 = (bf16[2,512,512]{2,1,0:T(8,128)(2,1)}, bf16[2,512,512]{2,1,0:T(8,128)(2,1)S(1)}, u32[]{:S(2)}) copy-start(bf16[2,512,512]{2,1,0:T(8,128)(2,1)S(1)} %select_dynamic-update-slice_fusion.2) | copy-start | bytes 3145732 | tf_op jit(solution)/shard_map/while
  280.8 3.6 copy-start.2
  297.5 14.3 %collective-permute-start = (bf16[1,512,512]{2,1,0:T(8,128)(2,1)S(1)}, bf16[1,512,512]{2,1,0:T(8,128)(2,1)S(1)}, u32[]{:S(2)}, u32[]{:S(2)}) collective-permute-start(bf16[1,512,512]{2,1,0:T(8,128)(2,1)S(1)} %get-tuple-element.521), channel_id=1, source_target_pairs={{32,0},{64,32},{96,64},{128,96},{160,128},{192,160},{224,192},{33,... | collective-permute-start | bytes 1572872 | tf_op jit(solution)/shard_map/while/body/eval_jaxpr/ppermute | solution.py:10
  299.4 11.2 %copy-start = (bf16[2,512,512]{2,1,0:T(8,128)(2,1)S(1)}, bf16[2,512,512]{2,1,0:T(8,128)(2,1)}, u32[]{:S(2)}) copy-start(bf16[2,512,512]{2,1,0:T(8,128)(2,1)} %get-tuple-element.544) | copy-start | bytes 3145732 | tf_op jit(solution)/shard_map/while
  311.8 3.6 copy-start.2
  328.5 13.3 %collective-permute-start = (bf16[1,512,512]{2,1,0:T(8,128)(2,1)S(1)}, bf16[1,512,512]{2,1,0:T(8,128)(2,1)S(1)}, u32[]{:S(2)}, u32[]{:S(2)}) collective-permute-start(bf16[1,512,512]{2,1,0:T(8,128)(2,1)S(1)} %get-tuple-element.521), channel_id=1, source_target_pairs={{32,0},{64,32},{96,64},{128,96},{160,128},{192,160},{224,192},{33,... | collective-permute-start | bytes 1572872 | tf_op jit(solution)/shard_map/while/body/eval_jaxpr/ppermute | solution.py:10
  330.5 11.2 %copy-start = (bf16[2,512,512]{2,1,0:T(8,128)(2,1)S(1)}, bf16[2,512,512]{2,1,0:T(8,128)(2,1)}, u32[]{:S(2)}) copy-start(bf16[2,512,512]{2,1,0:T(8,128)(2,1)} %get-tuple-element.544) | copy-start | bytes 3145732 | tf_op jit(solution)/shard_map/while
  347.2 21.9 %collective-permute-start = (bf16[1,512,512]{2,1,0:T(8,128)(2,1)S(1)}, bf16[1,512,512]{2,1,0:T(8,128)(2,1)S(1)}, u32[]{:S(2)}, u32[]{:S(2)}) collective-permute-start(bf16[1,512,512]{2,1,0:T(8,128)(2,1)S(1)} %get-tuple-element.521), channel_id=1, source_target_pairs={{32,0},{64,32},{96,64},{128,96},{160,128},{192,160},{224,192},{33,... | collective-permute-start | bytes 1572872 | tf_op jit(solution)/shard_map/while/body/eval_jaxpr/ppermute | solution.py:10
  357.7 11.2 %copy-start = (bf16[2,512,512]{2,1,0:T(8,128)(2,1)S(1)}, bf16[2,512,512]{2,1,0:T(8,128)(2,1)}, u32[]{:S(2)}) copy-start(bf16[2,512,512]{2,1,0:T(8,128)(2,1)} %get-tuple-element.544) | copy-start | bytes 3145732 | tf_op jit(solution)/shard_map/while
  374.4 13.3 %collective-permute-start = (bf16[1,512,512]{2,1,0:T(8,128)(2,1)S(1)}, bf16[1,512,512]{2,1,0:T(8,128)(2,1)S(1)}, u32[]{:S(2)}, u32[]{:S(2)}) collective-permute-start(bf16[1,512,512]{2,1,0:T(8,128)(2,1)S(1)} %get-tuple-element.521), channel_id=1, source_target_pairs={{32,0},{64,32},{96,64},{128,96},{160,128},{192,160},{224,192},{33,... | collective-permute-start | bytes 1572872 | tf_op jit(solution)/shard_map/while/body/eval_jaxpr/ppermute | solution.py:10
  376.3 11.2 %copy-start = (bf16[2,512,512]{2,1,0:T(8,128)(2,1)S(1)}, bf16[2,512,512]{2,1,0:T(8,128)(2,1)}, u32[]{:S(2)}) copy-start(bf16[2,512,512]{2,1,0:T(8,128)(2,1)} %get-tuple-element.544) | copy-start | bytes 3145732 | tf_op jit(solution)/shard_map/while
  (10 other events, 11.5 us)
Sparse Core Ops, SparseCore 0:
  10.6 79.3 all-gather.2
  92.6 76.8 all-gather.4
  397.8 227.0 reduce-scatter.1
where the time goes:
time: 635 us
  waiting for transfers between devices  410 us (65%)
  other arithmetic  116 us (18%)
  local copies, waits for them, and re-layouts  53.3 us (8%)
  starting transfers between devices  26.5 us (4%)
  matrix products  14.9 us (2%)
  between operations  13.8 us (2%)
    reduce_scatter x1, waiting for transfers between devices, local(): shares = lax.psum_scatter(grad_acc, 'dp', scatter_dimension=0, tiled=True)  227 us
    add x9, other arithmetic, step_fn(): grad_acc = grad_acc + grad_term  98.4 us
    all_gather x1, waiting for transfers between devices, local(): lax.all_gather(w_mix, 'dp', axis=1, tiled=True)  81.3 us
    all_gather x1, waiting for transfers between devices, local(): lax.all_gather(w_conv, 'dp', axis=1, tiled=True)  79.5 us
    another operation x15, local copies, waits for them, and re-layouts  30.4 us
    ppermute x9, starting transfers between devices, passed_along(): lax.ppermute(value, axis, [(source, source + steps) for source in range(l...  26.4 us
    ppermute x9, waiting for transfers between devices, passed_along(): lax.ppermute(value, axis, [(source, source + steps) for source in range(l...  20.7 us
  transfers between devices with their start and end apart: 12, of which 5 were waited for; matrix products, arithmetic and copies ran while one was open for 16% of the time, Pallas kernels for 0%

commit v1 on v0

--- a/solution.py
+++ b/solution.py
@@ -62,7 +62,9 @@
     sec_index = lax.axis_index("pipe")
     dilation = jnp.left_shift(jnp.int32(1), sec_index)
     conv_full, mix_full = (
-        lax.all_gather(w_conv, "dp", axis=1, tiled=True),
+        jnp.concatenate(
+            lax.all_to_all(jnp.stack([w_conv] * lax.axis_size("dp")), "dp", 0, 0), axis=1
+        ),
         lax.all_gather(w_mix, "dp", axis=1, tiled=True),
     )
     conv_w = conv_full[0]

time: 635 us -> 577 us (0.909)
  waiting for transfers between devices: 410 us -> 333 us
  starting transfers between devices: 26.5 us -> 38 us
  local copies, waits for them, and re-layouts: 53.3 us -> 60.5 us
    all_gather x1 -> x0, waiting for transfers between devices: 79.5 us -> none  [local(): lax.all_gather(w_conv, 'dp', axis=1, tiled=True)]
    all_to_all x0 -> x1, waiting for transfers between devices: none -> 76.1 us  [local(): lax.all_to_all(jnp.stack([w_conv] * lax.axis_size('dp')), 'dp', 0, 0)]
    all_gather x1, waiting for transfers between devices: 81.3 us -> 7.24 us  [local(): lax.all_gather(w_mix, 'dp', axis=1, tiled=True)]
    all_to_all x0 -> x1, starting transfers between devices: none -> 11.6 us  [local(): lax.all_to_all(jnp.stack([w_conv] * lax.axis_size('dp')), 'dp', 0, 0)]
    another operation x15 -> x16, local copies, waits for them, and re-layouts: 30.4 us -> 33.5 us
  transfers between devices with their start and end apart: 12 -> 12, of which waited for: 5 -> 5; matrix products, arithmetic and copies ran while one was open for 16% -> 18% of each run, Pallas kernels for 0% -> 0%
where the time goes in v1:
time: 577 us
  waiting for transfers between devices  333 us (58%)
  other arithmetic  116 us (20%)
  local copies, waits for them, and re-layouts  60.5 us (10%)
  starting transfers between devices  38 us (7%)
  matrix products  15 us (3%)
  between operations  14.1 us (2%)
    reduce_scatter x1, waiting for transfers between devices, local(): shares = lax.psum_scatter(grad_acc, 'dp', scatter_dimension=0, tiled=True)  228 us
    add x9, other arithmetic, step_fn(): grad_acc = grad_acc + grad_term  98.5 us
    all_to_all x1, waiting for transfers between devices, local(): lax.all_to_all(jnp.stack([w_conv] * lax.axis_size('dp')), 'dp', 0, 0)  76.1 us
    another operation x15, local copies, waits for them, and re-layouts  30.5 us
    ppermute x9, starting transfers between devices, passed_along(): lax.ppermute(value, axis, [(source, source + steps) for source in range(l...  26.3 us
    ppermute x9, waiting for transfers between devices, passed_along(): lax.ppermute(value, axis, [(source, source + steps) for source in range(l...  20.9 us
    all_to_all x1, starting transfers between devices, local(): lax.all_to_all(jnp.stack([w_conv] * lax.axis_size('dp')), 'dp', 0, 0)  11.6 us
  transfers between devices with their start and end apart: 12, of which 5 were waited for; matrix products, arithmetic and copies ran while one was open for 18% of the time, Pallas kernels for 0%

profile of v1, /device:TPU:2, one launch (start us, length us, event | category | flops | bytes accessed | tf_op | source)
XLA Modules:
  0.0 576.8 jit_solution(16075663190200414000)
XLA Ops:
  10.2 11.6 %all-to-all-start = ((bf16[32,1,16,3,1024]{4,2,3,1,0:T(8,128)(2,1)}), bf16[32,1,16,3,1024]{4,2,3,1,0:T(8,128)(2,1)}, u32[]{:S(2)}, u32[]{:S(2)}) async-start(bf16[32,1,16,3,1024]{4,2,3,1,0:T(8,128)(2,1)} %stack.18), calls=%async_computation | async-start | bytes 6291456 | tf_op jit(solution)/shard_map/all_to_all | solution.py:66
  22.6 76.1 %all-to-all-done = bf16[32,1,16,3,1024]{4,2,3,1,0:T(8,128)(2,1)} async-done(((bf16[32,1,16,3,1024]{4,2,3,1,0:T(8,128)(2,1)}), bf16[32,1,16,3,1024]{4,2,3,1,0:T(8,128)(2,1)}, u32[]{:S(2)}, u32[]{:S(2)}) %all-to-all-start) | async-done | bytes 3145760 | tf_op jit(solution)/shard_map/all_to_all | solution.py:66
  102.8 7.2 %all-gather.2.cloned.1.call-done = bf16[1,512,1024]{2,1,0:T(8,128)(2,1)} async-done(((bf16[1,16,1024]{2,1,0:T(8,128)(2,1)}), bf16[1,512,1024]{2,1,0:T(8,128)(2,1)}) %all-gather.2.cloned.1.call-update) | async-done | bytes 1048592 | tf_op jit(solution)/shard_map/all_gather | solution.py:68
  111.2 218.4 %while.20 = (s32[]{:T(128)}, bf16[1,512,512]{2,1,0:T(8,128)(2,1)S(1)}, bf16[2,512,512]{2,1,0:T(8,128)(2,1)}, f32[512,4096]{0,1:T(8,128)}, s32[]{:T(128)}, /*inde...) while((s32[]{:T(128)}, ...), condition=%wide.region_3.8_spmd.clone, body=%wide.region_0.7_spmd.clone.sunk | while | flops 5937039872 | bytes 117971056 | solution.py:131
  111.2 4.4 conditional.3
  117.4 8.8 %select_add_fusion.2 = f32[512,4096]{0,1:T(8,128)} fusion(f32[512,4096]{0,1:T(8,128)} %get-tuple-element.528, f32[512,4096]{0,1:T(8,128)} %get-tuple-element.551, pred[]{:T(512)S(6)} %compare.5), kind=kLoop, calls=%fused_computation.59.clone.1 | loop fusion | flops 4194304 | bytes 25165824 | tf_op jit(solution)/shard_map/while/body/eval_jaxpr/add | solution.py:114
  127.4 4.4 conditional.3
  134.2 11.2 %select_add_fusion.2 = f32[512,4096]{0,1:T(8,128)} fusion(f32[512,4096]{0,1:T(8,128)} %get-tuple-element.528, f32[512,4096]{0,1:T(8,128)} %get-tuple-element.551, pred[]{:T(512)S(6)} %compare.5), kind=kLoop, calls=%fused_computation.59.clone.1 | loop fusion | flops 4194304 | bytes 25165824 | tf_op jit(solution)/shard_map/while/body/eval_jaxpr/add | solution.py:114
  146.6 4.4 conditional.3
  152.9 11.2 %select_add_fusion.2 = f32[512,4096]{0,1:T(8,128)} fusion(f32[512,4096]{0,1:T(8,128)} %get-tuple-element.528, f32[512,4096]{0,1:T(8,128)} %get-tuple-element.551, pred[]{:T(512)S(6)} %compare.5), kind=kLoop, calls=%fused_computation.59.clone.1 | loop fusion | flops 4194304 | bytes 25165824 | tf_op jit(solution)/shard_map/while/body/eval_jaxpr/add | solution.py:114
  165.2 4.4 conditional.3
  171.5 11.2 %select_add_fusion.2 = f32[512,4096]{0,1:T(8,128)} fusion(f32[512,4096]{0,1:T(8,128)} %get-tuple-element.528, f32[512,4096]{0,1:T(8,128)} %get-tuple-element.551, pred[]{:T(512)S(6)} %compare.5), kind=kLoop, calls=%fused_computation.59.clone.1 | loop fusion | flops 4194304 | bytes 25165824 | tf_op jit(solution)/shard_map/while/body/eval_jaxpr/add | solution.py:114
  183.9 4.4 conditional.3
  190.2 11.2 %select_add_fusion.2 = f32[512,4096]{0,1:T(8,128)} fusion(f32[512,4096]{0,1:T(8,128)} %get-tuple-element.528, f32[512,4096]{0,1:T(8,128)} %get-tuple-element.551, pred[]{:T(512)S(6)} %compare.5), kind=kLoop, calls=%fused_computation.59.clone.1 | loop fusion | flops 4194304 | bytes 25165824 | tf_op jit(solution)/shard_map/while/body/eval_jaxpr/add | solution.py:114
  201.6 20.0 %collective-permute-done = bf16[1,512,512]{2,1,0:T(8,128)(2,1)S(1)} collective-permute-done((bf16[1,512,512]{2,1,0:T(8,128)(2,1)S(1)}, bf16[1,512,512]{2,1,0:T(8,128)(2,1)S(1)}, u32[]{:S(2)}, u32[]{:S(2)}) %collective-permute-start) | collective-permute-done | bytes 524320 | tf_op jit(solution)/shard_map/while/body/eval_jaxpr/ppermute | solution.py:10
  221.6 16.8 %conditional.3 = (bf16[1,512,512]{2,1,0:T(8,128)(2,1)S(1)}, f32[512,4096]{0,1:T(8,128)}) conditional(s32[]{:T(128)} %convert_element_type.39, () %tuple.73, (pred[]{:T(512)}, bf16[2,512,512]{2,1,0:T(8,128)(2,1)}, s32[]{:T(128)}, bf16[1,512,512]{2,1,0:T(8,128)(2,1)S(1)}, bf16[2,512,512]{2,1,0:T(8,128)(2,1)}, /*index=5*/bf16[512,1024]{1,0:T(8,128)(2,1)}, ...), branch_computations={%region_1.1_spmd, %region_2.6_spmd} | conditional | flops 5932583424 | bytes 80746224 | solution.py:113
  240.3 11.2 %select_add_fusion.2 = f32[512,4096]{0,1:T(8,128)} fusion(f32[512,4096]{0,1:T(8,128)} %get-tuple-element.528, f32[512,4096]{0,1:T(8,128)} %get-tuple-element.551, pred[]{:T(512)S(6)} %compare.5), kind=kLoop, calls=%fused_computation.59.clone.1 | loop fusion | flops 4194304 | bytes 25165824 | tf_op jit(solution)/shard_map/while/body/eval_jaxpr/add | solution.py:114
  252.6 16.8 %conditional.3 = (bf16[1,512,512]{2,1,0:T(8,128)(2,1)S(1)}, f32[512,4096]{0,1:T(8,128)}) conditional(s32[]{:T(128)} %convert_element_type.39, () %tuple.73, (pred[]{:T(512)}, bf16[2,512,512]{2,1,0:T(8,128)(2,1)}, s32[]{:T(128)}, bf16[1,512,512]{2,1,0:T(8,128)(2,1)S(1)}, bf16[2,512,512]{2,1,0:T(8,128)(2,1)}, /*index=5*/bf16[512,1024]{1,0:T(8,128)(2,1)}, ...), branch_computations={%region_1.1_spmd, %region_2.6_spmd} | conditional | flops 5932583424 | bytes 80746224 | solution.py:113
  271.3 11.2 %select_add_fusion.2 = f32[512,4096]{0,1:T(8,128)} fusion(f32[512,4096]{0,1:T(8,128)} %get-tuple-element.528, f32[512,4096]{0,1:T(8,128)} %get-tuple-element.551, pred[]{:T(512)S(6)} %compare.5), kind=kLoop, calls=%fused_computation.59.clone.1 | loop fusion | flops 4194304 | bytes 25165824 | tf_op jit(solution)/shard_map/while/body/eval_jaxpr/add | solution.py:114
  288.0 10.5 %collective-permute-start = (bf16[1,512,512]{2,1,0:T(8,128)(2,1)S(1)}, bf16[1,512,512]{2,1,0:T(8,128)(2,1)S(1)}, u32[]{:S(2)}, u32[]{:S(2)}) collective-permute-start(bf16[1,512,512]{2,1,0:T(8,128)(2,1)S(1)} %get-tuple-element.527), channel_id=1, source_target_pairs={{32,0},{64,32},{96,64},{128,96},{160,128},{192,160},{224,192},{33,... | collective-permute-start | bytes 1572872 | tf_op jit(solution)/shard_map/while/body/eval_jaxpr/ppermute | solution.py:10
  298.6 11.2 %select_add_fusion.2 = f32[512,4096]{0,1:T(8,128)} fusion(f32[512,4096]{0,1:T(8,128)} %get-tuple-element.528, f32[512,4096]{0,1:T(8,128)} %get-tuple-element.551, pred[]{:T(512)S(6)} %compare.5), kind=kLoop, calls=%fused_computation.59.clone.1 | loop fusion | flops 4194304 | bytes 25165824 | tf_op jit(solution)/shard_map/while/body/eval_jaxpr/add | solution.py:114
  317.2 11.2 %select_add_fusion.2 = f32[512,4096]{0,1:T(8,128)} fusion(f32[512,4096]{0,1:T(8,128)} %get-tuple-element.528, f32[512,4096]{0,1:T(8,128)} %get-tuple-element.551, pred[]{:T(512)S(6)} %compare.5), kind=kLoop, calls=%fused_computation.59.clone.1 | loop fusion | flops 4194304 | bytes 25165824 | tf_op jit(solution)/shard_map/while/body/eval_jaxpr/add | solution.py:114
  329.6 8.9 %copy.26 = f32[512,4096]{1,0:T(8,128)} copy(f32[512,4096]{0,1:T(8,128)} %get-tuple-element.365) | data formatting | bytes 16777216 | tf_op jit(solution)/shard_map/while | solution.py:131
  338.5 228.1 %reduce-scatter.2.cloned.1.call-done = f32[16,4096]{1,0:T(8,128)} async-done(((f32[512,4096]{1,0:T(8,128)}), f32[16,4096]{1,0:T(8,128)}) %reduce-scatter.2.cloned.1.call-update) | async-done | bytes 262160 | tf_op jit(solution)/shard_map/reduce_scatter | solution.py:134
  (126 shorter events, 109.9 us)
Async XLA Ops:
  10.2 88.5 %all-to-all-start = ((bf16[32,1,16,3,1024]{4,2,3,1,0:T(8,128)(2,1)}), bf16[32,1,16,3,1024]{4,2,3,1,0:T(8,128)(2,1)}, u32[]{:S(2)}, u32[]{:S(2)}) async-start(bf16[32,1,16,3,1024]{4,2,3,1,0:T(8,128)(2,1)} %stack.18), calls=%async_computation | async-start | bytes 6291456 | tf_op jit(solution)/shard_map/all_to_all | solution.py:66
  21.8 88.3 %all-gather.2.cloned.1.call-start = ((), (), s32[]{:S(2)}) async-start(), calls=%async_computation.2 | async-start | bytes 1081344 | tf_op jit(solution)/shard_map/all_gather | solution.py:68
  22.5 544.1 %reduce-scatter.2.cloned.1.call-start = ((), (), s32[]{:S(2)}) async-start(), calls=%async_computation.3 | async-start | bytes 8650752 | tf_op jit(solution)/shard_map/reduce_scatter | solution.py:134
  115.5 11.0 %collective-permute-start = (bf16[1,512,512]{2,1,0:T(8,128)(2,1)S(1)}, bf16[1,512,512]{2,1,0:T(8,128)(2,1)S(1)}, u32[]{:S(2)}, u32[]{:S(2)}) collective-permute-start(bf16[1,512,512]{2,1,0:T(8,128)(2,1)S(1)} %get-tuple-element.527), channel_id=1, source_target_pairs={{32,0},{64,32},{96,64},{128,96},{160,128},{192,160},{224,192},{33,... | collective-permute-start | bytes 1572872 | tf_op jit(solution)/shard_map/while/body/eval_jaxpr/ppermute | solution.py:10
  117.4 8.9 %copy-start = (bf16[2,512,512]{2,1,0:T(8,128)(2,1)S(1)}, bf16[2,512,512]{2,1,0:T(8,128)(2,1)}, u32[]{:S(2)}) copy-start(bf16[2,512,512]{2,1,0:T(8,128)(2,1)} %get-tuple-element.550) | copy-start | bytes 3145732 | tf_op jit(solution)/shard_map/while
  131.8 13.8 %collective-permute-start = (bf16[1,512,512]{2,1,0:T(8,128)(2,1)S(1)}, bf16[1,512,512]{2,1,0:T(8,128)(2,1)S(1)}, u32[]{:S(2)}, u32[]{:S(2)}) collective-permute-start(bf16[1,512,512]{2,1,0:T(8,128)(2,1)S(1)} %get-tuple-element.527), channel_id=1, source_target_pairs={{32,0},{64,32},{96,64},{128,96},{160,128},{192,160},{224,192},{33,... | collective-permute-start | bytes 1572872 | tf_op jit(solution)/shard_map/while/body/eval_jaxpr/ppermute | solution.py:10
  134.2 11.2 %copy-start = (bf16[2,512,512]{2,1,0:T(8,128)(2,1)S(1)}, bf16[2,512,512]{2,1,0:T(8,128)(2,1)}, u32[]{:S(2)}) copy-start(bf16[2,512,512]{2,1,0:T(8,128)(2,1)} %get-tuple-element.550) | copy-start | bytes 3145732 | tf_op jit(solution)/shard_map/while
  150.9 13.3 %collective-permute-start = (bf16[1,512,512]{2,1,0:T(8,128)(2,1)S(1)}, bf16[1,512,512]{2,1,0:T(8,128)(2,1)S(1)}, u32[]{:S(2)}, u32[]{:S(2)}) collective-permute-start(bf16[1,512,512]{2,1,0:T(8,128)(2,1)S(1)} %get-tuple-element.527), channel_id=1, source_target_pairs={{32,0},{64,32},{96,64},{128,96},{160,128},{192,160},{224,192},{33,... | collective-permute-start | bytes 1572872 | tf_op jit(solution)/shard_map/while/body/eval_jaxpr/ppermute | solution.py:10
  152.9 11.2 %copy-start = (bf16[2,512,512]{2,1,0:T(8,128)(2,1)S(1)}, bf16[2,512,512]{2,1,0:T(8,128)(2,1)}, u32[]{:S(2)}) copy-start(bf16[2,512,512]{2,1,0:T(8,128)(2,1)} %get-tuple-element.550) | copy-start | bytes 3145732 | tf_op jit(solution)/shard_map/while
  169.6 13.3 %collective-permute-start = (bf16[1,512,512]{2,1,0:T(8,128)(2,1)S(1)}, bf16[1,512,512]{2,1,0:T(8,128)(2,1)S(1)}, u32[]{:S(2)}, u32[]{:S(2)}) collective-permute-start(bf16[1,512,512]{2,1,0:T(8,128)(2,1)S(1)} %get-tuple-element.527), channel_id=1, source_target_pairs={{32,0},{64,32},{96,64},{128,96},{160,128},{192,160},{224,192},{33,... | collective-permute-start | bytes 1572872 | tf_op jit(solution)/shard_map/while/body/eval_jaxpr/ppermute | solution.py:10
  171.5 11.2 %copy-start = (bf16[2,512,512]{2,1,0:T(8,128)(2,1)S(1)}, bf16[2,512,512]{2,1,0:T(8,128)(2,1)}, u32[]{:S(2)}) copy-start(bf16[2,512,512]{2,1,0:T(8,128)(2,1)} %get-tuple-element.550) | copy-start | bytes 3145732 | tf_op jit(solution)/shard_map/while
  188.2 33.3 %collective-permute-start = (bf16[1,512,512]{2,1,0:T(8,128)(2,1)S(1)}, bf16[1,512,512]{2,1,0:T(8,128)(2,1)S(1)}, u32[]{:S(2)}, u32[]{:S(2)}) collective-permute-start(bf16[1,512,512]{2,1,0:T(8,128)(2,1)S(1)} %get-tuple-element.527), channel_id=1, source_target_pairs={{32,0},{64,32},{96,64},{128,96},{160,128},{192,160},{224,192},{33,... | collective-permute-start | bytes 1572872 | tf_op jit(solution)/shard_map/while/body/eval_jaxpr/ppermute | solution.py:10
  190.1 11.2 %copy-start = (bf16[2,512,512]{2,1,0:T(8,128)(2,1)S(1)}, bf16[2,512,512]{2,1,0:T(8,128)(2,1)}, u32[]{:S(2)}) copy-start(bf16[2,512,512]{2,1,0:T(8,128)(2,1)} %get-tuple-element.550) | copy-start | bytes 3145732 | tf_op jit(solution)/shard_map/while
  201.6 20.0 %copy-start.1 = (bf16[2,512,512]{2,1,0:T(8,128)(2,1)}, bf16[2,512,512]{2,1,0:T(8,128)(2,1)S(1)}, u32[]{:S(2)}) copy-start(bf16[2,512,512]{2,1,0:T(8,128)(2,1)S(1)} %select_dynamic-update-slice_fusion.2) | copy-start | bytes 3145732 | tf_op jit(solution)/shard_map/while
  221.6 3.6 copy-start.2
  238.3 14.3 %collective-permute-start = (bf16[1,512,512]{2,1,0:T(8,128)(2,1)S(1)}, bf16[1,512,512]{2,1,0:T(8,128)(2,1)S(1)}, u32[]{:S(2)}, u32[]{:S(2)}) collective-permute-start(bf16[1,512,512]{2,1,0:T(8,128)(2,1)S(1)} %get-tuple-element.527), channel_id=1, source_target_pairs={{32,0},{64,32},{96,64},{128,96},{160,128},{192,160},{224,192},{33,... | collective-permute-start | bytes 1572872 | tf_op jit(solution)/shard_map/while/body/eval_jaxpr/ppermute | solution.py:10
  240.2 11.2 %copy-start = (bf16[2,512,512]{2,1,0:T(8,128)(2,1)S(1)}, bf16[2,512,512]{2,1,0:T(8,128)(2,1)}, u32[]{:S(2)}) copy-start(bf16[2,512,512]{2,1,0:T(8,128)(2,1)} %get-tuple-element.550) | copy-start | bytes 3145732 | tf_op jit(solution)/shard_map/while
  252.6 3.6 copy-start.2
  269.4 13.3 %collective-permute-start = (bf16[1,512,512]{2,1,0:T(8,128)(2,1)S(1)}, bf16[1,512,512]{2,1,0:T(8,128)(2,1)S(1)}, u32[]{:S(2)}, u32[]{:S(2)}) collective-permute-start(bf16[1,512,512]{2,1,0:T(8,128)(2,1)S(1)} %get-tuple-element.527), channel_id=1, source_target_pairs={{32,0},{64,32},{96,64},{128,96},{160,128},{192,160},{224,192},{33,... | collective-permute-start | bytes 1572872 | tf_op jit(solution)/shard_map/while/body/eval_jaxpr/ppermute | solution.py:10
  271.3 11.2 %copy-start = (bf16[2,512,512]{2,1,0:T(8,128)(2,1)S(1)}, bf16[2,512,512]{2,1,0:T(8,128)(2,1)}, u32[]{:S(2)}) copy-start(bf16[2,512,512]{2,1,0:T(8,128)(2,1)} %get-tuple-element.550) | copy-start | bytes 3145732 | tf_op jit(solution)/shard_map/while
  288.0 22.0 %collective-permute-start = (bf16[1,512,512]{2,1,0:T(8,128)(2,1)S(1)}, bf16[1,512,512]{2,1,0:T(8,128)(2,1)S(1)}, u32[]{:S(2)}, u32[]{:S(2)}) collective-permute-start(bf16[1,512,512]{2,1,0:T(8,128)(2,1)S(1)} %get-tuple-element.527), channel_id=1, source_target_pairs={{32,0},{64,32},{96,64},{128,96},{160,128},{192,160},{224,192},{33,... | collective-permute-start | bytes 1572872 | tf_op jit(solution)/shard_map/while/body/eval_jaxpr/ppermute | solution.py:10
  298.6 11.2 %copy-start = (bf16[2,512,512]{2,1,0:T(8,128)(2,1)S(1)}, bf16[2,512,512]{2,1,0:T(8,128)(2,1)}, u32[]{:S(2)}) copy-start(bf16[2,512,512]{2,1,0:T(8,128)(2,1)} %get-tuple-element.550) | copy-start | bytes 3145732 | tf_op jit(solution)/shard_map/while
  315.3 13.3 %collective-permute-start = (bf16[1,512,512]{2,1,0:T(8,128)(2,1)S(1)}, bf16[1,512,512]{2,1,0:T(8,128)(2,1)S(1)}, u32[]{:S(2)}, u32[]{:S(2)}) collective-permute-start(bf16[1,512,512]{2,1,0:T(8,128)(2,1)S(1)} %get-tuple-element.527), channel_id=1, source_target_pairs={{32,0},{64,32},{96,64},{128,96},{160,128},{192,160},{224,192},{33,... | collective-permute-start | bytes 1572872 | tf_op jit(solution)/shard_map/while/body/eval_jaxpr/ppermute | solution.py:10
  317.2 11.2 %copy-start = (bf16[2,512,512]{2,1,0:T(8,128)(2,1)S(1)}, bf16[2,512,512]{2,1,0:T(8,128)(2,1)}, u32[]{:S(2)}) copy-start(bf16[2,512,512]{2,1,0:T(8,128)(2,1)} %get-tuple-element.550) | copy-start | bytes 3145732 | tf_op jit(solution)/shard_map/while
  (10 other events, 11.5 us)
Sparse Core Ops, SparseCore 0:
  25.2 84.8 all-gather.1
  338.7 227.8 reduce-scatter.1
